TPU v7x, 512 devices: a whole 4x8x8 slice. The times are simulated.
512 devices in a mesh: tm: 64 (over z_hi, x, y), space: 8 (over z_lo, core).
Axes of the slice: x: 4, y: 8, z: 8 (z_hi: 2, z_lo: 4; z = z_hi * 4 + z_lo), core: 2. Of those that a mesh axis runs over, the one named last changes fastest.
Arguments:
- start_states: float32 [64, 128, 16, 128], P('tm', 'space'), may hold values from -6 to 6
- material: int32 [128, 16, 128], P('space'), may hold values from 0 to 15
- source: float32 [128, 16, 128], P('space'), may hold values from -0.6 to 0.6
- conductivity: float32 [16], replicated, may hold values from 0.02 to 0.16
- tide_amp: float32 [12], replicated, may hold values from -1.5 to 1.5
- phase: int32 [64], P('tm'), may hold values from 0 to 11
- coarse_rate: float32 [32, 4, 32], P('space'), may hold values from 0.3 to 40
Outputs:
- final_states: float32 [64, 128, 16, 128], P('tm', 'space')
All inputs are finite; a program needn't handle non-finite values.
Results may differ from a plain program's by a relative error of at most 0.00013.
Values sent between devices are 32-bit elements; how exact they have to be, the bound alone decides.
A program may use at most 64 MiB of HBM per device.

v0:
```python
import jax
import jax.numpy as jnp
from jax import lax
from jax.sharding import PartitionSpec as P

FINE = 10
ITERS = 2


def padded_2(block, sides, width):
    for axis, dim in sides:
        count = lax.axis_size(axis)
        forward = [(i, i + 1) for i in range(count - 1)]
        backward = [(target, source) for source, target in forward]
        low = lax.ppermute(
            lax.slice_in_dim(block, block.shape[dim] - width, None, axis=dim), axis, forward
        )
        high = lax.ppermute(lax.slice_in_dim(block, 0, width, axis=dim), axis, backward)
        block = jnp.concatenate([low, block, high], axis=dim)
    return block


def from_behind(block, axis, distance):
    devices = range(lax.axis_size(axis))
    route = [((i - distance) % len(devices), i) for i in devices]
    return lax.ppermute(block, axis, route)


def lookup_coef(material, conductivity):
    result = jnp.zeros(material.shape, jnp.float32)
    for class_id in range(conductivity.shape[0]):
        result = jnp.where(material == class_id, conductivity[class_id], result)
    return result


def neighbour_total(padded):
    framed = jnp.pad(padded, ((0, 0), (1, 1), (1, 1)))
    total = framed[2:, 1:-1, 1:-1] + framed[:-2, 1:-1, 1:-1]
    total = total + framed[1:-1, 2:, 1:-1] + framed[1:-1, :-2, 1:-1]
    total = total + framed[1:-1, 1:-1, 2:] + framed[1:-1, 1:-1, :-2]
    return total


def slab_update(field_now, cell_coef, forcing):
    padded = padded_2(field_now, (("space", 0),), 1)
    neighbours = neighbour_total(padded)
    return field_now + cell_coef * (neighbours - 6.0 * field_now) + forcing


def restrict(field_now):
    depth, rows, cols = field_now.shape
    blocks = field_now.reshape((depth // 4, 4, rows // 4, 4, cols // 4, 4))
    return blocks.mean(axis=(1, 3, 5))


def prolong(coarse):
    depth, rows, cols = coarse.shape
    wide = jnp.broadcast_to(coarse[:, None, :, None, :, None], (depth, 4, rows, 4, cols, 4))
    return wide.reshape((depth * 4, rows * 4, cols * 4))


def body(start_states, material, source, conductivity, tide_amp, phase, coarse_rate):
    windows = lax.axis_size("tm")
    device_index = lax.axis_index("tm")
    cell_coef = lookup_coef(material, conductivity)
    phase_ids = jnp.arange(tide_amp.shape[0], dtype=jnp.int32)
    decay = jnp.exp(-coarse_rate / windows)
    closure = 1.0 - jnp.exp(-coarse_rate)
    field_now = start_states[0]
    for outer in range(ITERS):
        tide_level = jnp.sum(jnp.where(phase_ids == phase[0], tide_amp, 0.0))
        forcing = tide_level * source
        finish = field_now
        for substep in range(FINE):
            finish = slab_update(finish, cell_coef, forcing)
        coarse_start = restrict(field_now)
        jump_now = restrict(finish) - decay * coarse_start
        pieces = lax.all_gather(jump_now[None], "tm", axis=0, tiled=True)
        count = pieces.shape[0]
        seen = jnp.arange(count, dtype=jnp.int32)
        lagged = (device_index - 1 - seen) % windows
        weights = jnp.exp(
            -coarse_rate[None] * lagged.astype(jnp.float32)[:, None, None, None] / windows
        )
        gathered_sum = jnp.sum(weights * pieces, axis=0)
        coarse = gathered_sum / closure
        corrected = finish + prolong(decay * (coarse - coarse_start))
        field_now = from_behind(corrected, "tm", 1)
    return field_now[None]


def solution(mesh):
    placed = (
        P("tm", "space", None, None),
        P("space", None, None),
        P("space", None, None),
        P(),
        P(),
        P("tm"),
        P("space", None, None),
    )
    return jax.shard_map(
        body, mesh=mesh, in_specs=placed, out_specs=P("tm", "space", None, None), check_vma=False
    )
```

profile of v0, /device:TPU:64, one launch (start us, length us, event | category | flops | bytes accessed | tf_op | source)
XLA Modules:
  0.0 887.4 jit_solution(9521776563705246436)
XLA Ops:
  11.3 11.9 %fusion.101 = f32[16,16,128]{2,1,0:T(8,128)S(1)} fusion(f32[16,16,128]{2,1,0:T(8,128)} %bitcast.35, f32[18,18,130]{2,1,0:T(8,128)S(1)} %select_maximum_fusion.38, f32[1,16,128]{2,1,0:T(8,128)S(1)} %collective-permute-done.1, f32[1,16,128]{2,1,0:T(8,128)S(1)} %collective-permute-done, f32[16,16,128]{2,1,0:T(8,128)} %param.9, f32[]{:T(128)} %fusion.103, ...), kind=kLoop, calls=%fused_computation.263 | loop fusion | flops 1474560 | bytes 1065028 | tf_op jit(solution)/shard_map/add | solution.py:47
  31.4 11.8 %fusion.96 = f32[16,16,128]{2,1,0:T(8,128)S(1)} fusion(f32[16,16,128]{2,1,0:T(8,128)S(1)} %fusion.101, f32[18,18,130]{2,1,0:T(8,128)S(1)} %select_maximum_fusion.36, f32[1,16,128]{2,1,0:T(8,128)S(1)} %collective-permute-done.3, f32[1,16,128]{2,1,0:T(8,128)S(1)} %collective-permute-done.2, f32[16,16,128]{2,1,0:T(8,128)} %param.9, f32[]{:T(128)} %fusion.103, ...), kind=kLoop, calls=%fused_computation.252 | loop fusion | flops 1474560 | bytes 1065028 | tf_op jit(solution)/shard_map/add | solution.py:47
  50.3 10.8 %fusion.91 = f32[16,16,128]{2,1,0:T(8,128)S(1)} fusion(f32[16,16,128]{2,1,0:T(8,128)S(1)} %fusion.96, f32[18,18,130]{2,1,0:T(8,128)S(1)} %select_maximum_fusion.34, f32[1,16,128]{2,1,0:T(8,128)S(1)} %collective-permute-done.5, f32[1,16,128]{2,1,0:T(8,128)S(1)} %collective-permute-done.4, f32[16,16,128]{2,1,0:T(8,128)S(1)} %copy-done, f32[]{:T(128)} %fusion.103, ...), kind=kLoop, calls=%fused_computation.241 | loop fusion | flops 1474560 | bytes 1065028 | tf_op jit(solution)/shard_map/add | solution.py:47
  68.6 10.8 %fusion.86 = f32[16,16,128]{2,1,0:T(8,128)S(1)} fusion(f32[16,16,128]{2,1,0:T(8,128)S(1)} %fusion.91, f32[18,18,130]{2,1,0:T(8,128)S(1)} %select_maximum_fusion.32, f32[1,16,128]{2,1,0:T(8,128)S(1)} %collective-permute-done.7, f32[1,16,128]{2,1,0:T(8,128)S(1)} %collective-permute-done.6, f32[16,16,128]{2,1,0:T(8,128)S(1)} %copy-done, f32[]{:T(128)} %fusion.103, ...), kind=kLoop, calls=%fused_computation.230 | loop fusion | flops 1474560 | bytes 1065028 | tf_op jit(solution)/shard_map/add | solution.py:47
  86.7 10.8 %fusion.81 = f32[16,16,128]{2,1,0:T(8,128)S(1)} fusion(f32[16,16,128]{2,1,0:T(8,128)S(1)} %fusion.86, f32[18,18,130]{2,1,0:T(8,128)S(1)} %select_maximum_fusion.30, f32[1,16,128]{2,1,0:T(8,128)S(1)} %collective-permute-done.9, f32[1,16,128]{2,1,0:T(8,128)S(1)} %collective-permute-done.8, f32[16,16,128]{2,1,0:T(8,128)S(1)} %copy-done, f32[]{:T(128)} %fusion.103, ...), kind=kLoop, calls=%fused_computation.219 | loop fusion | flops 1474560 | bytes 1065028 | tf_op jit(solution)/shard_map/add | solution.py:47
  104.6 10.8 %fusion.76 = f32[16,16,128]{2,1,0:T(8,128)S(1)} fusion(f32[16,16,128]{2,1,0:T(8,128)S(1)} %fusion.81, f32[18,18,130]{2,1,0:T(8,128)S(1)} %select_maximum_fusion.28, f32[1,16,128]{2,1,0:T(8,128)S(1)} %collective-permute-done.11, f32[1,16,128]{2,1,0:T(8,128)S(1)} %collective-permute-done.10, f32[16,16,128]{2,1,0:T(8,128)S(1)} %copy-done, f32[]{:T(128)} %fusion.103, ...), kind=kLoop, calls=%fused_computation.208 | loop fusion | flops 1474560 | bytes 1065028 | tf_op jit(solution)/shard_map/add | solution.py:47
  122.6 10.8 %fusion.71 = f32[16,16,128]{2,1,0:T(8,128)S(1)} fusion(f32[16,16,128]{2,1,0:T(8,128)S(1)} %fusion.76, f32[18,18,130]{2,1,0:T(8,128)S(1)} %select_maximum_fusion.26, f32[1,16,128]{2,1,0:T(8,128)S(1)} %collective-permute-done.13, f32[1,16,128]{2,1,0:T(8,128)S(1)} %collective-permute-done.12, f32[16,16,128]{2,1,0:T(8,128)S(1)} %copy-done, f32[]{:T(128)} %fusion.103, ...), kind=kLoop, calls=%fused_computation.197 | loop fusion | flops 1474560 | bytes 1065028 | tf_op jit(solution)/shard_map/add | solution.py:47
  140.5 10.8 %fusion.66 = f32[16,16,128]{2,1,0:T(8,128)S(1)} fusion(f32[16,16,128]{2,1,0:T(8,128)S(1)} %fusion.71, f32[18,18,130]{2,1,0:T(8,128)S(1)} %select_maximum_fusion.24, f32[1,16,128]{2,1,0:T(8,128)S(1)} %collective-permute-done.15, f32[1,16,128]{2,1,0:T(8,128)S(1)} %collective-permute-done.14, f32[16,16,128]{2,1,0:T(8,128)S(1)} %copy-done, f32[]{:T(128)} %fusion.103, ...), kind=kLoop, calls=%fused_computation.186 | loop fusion | flops 1474560 | bytes 1065028 | tf_op jit(solution)/shard_map/add | solution.py:47
  158.4 10.8 %fusion.61 = f32[16,16,128]{2,1,0:T(8,128)S(1)} fusion(f32[16,16,128]{2,1,0:T(8,128)S(1)} %fusion.66, f32[18,18,130]{2,1,0:T(8,128)S(1)} %select_maximum_fusion.22, f32[1,16,128]{2,1,0:T(8,128)S(1)} %collective-permute-done.17, f32[1,16,128]{2,1,0:T(8,128)S(1)} %collective-permute-done.16, f32[16,16,128]{2,1,0:T(8,128)S(1)} %copy-done, f32[]{:T(128)} %fusion.103, ...), kind=kLoop, calls=%fused_computation.175 | loop fusion | flops 1474560 | bytes 1065028 | tf_op jit(solution)/shard_map/add | solution.py:47
  183.3 10.8 %fusion.56 = f32[16,16,128]{2,1,0:T(8,128)S(1)} fusion(f32[16,16,128]{2,1,0:T(8,128)S(1)} %fusion.61, f32[18,18,130]{2,1,0:T(8,128)S(1)} %select_maximum_fusion.20, f32[1,16,128]{2,1,0:T(8,128)S(1)} %collective-permute-done.19, f32[1,16,128]{2,1,0:T(8,128)S(1)} %collective-permute-done.18, f32[16,16,128]{2,1,0:T(8,128)S(1)} %copy-done, f32[]{:T(128)} %fusion.103, ...), kind=kLoop, calls=%fused_computation.164 | loop fusion | flops 1474560 | bytes 1065028 | tf_op jit(solution)/shard_map/add | solution.py:47
  202.5 227.3 %all-gather = f32[256,4,32]{2,1,0:T(4,128)S(1)} all-gather(f32[4,4,32]{2,1,0:T(4,128)S(1)} %get-tuple-element.46), channel_id=2, replica_groups=mesh['tm'=64,'space'=8] {'tm'}, dimensions={0}, use_global_device_ids=true | all-gather | bytes 133120 | tf_op jit(solution)/shard_map/all_gather | solution.py:78
  439.5 13.1 %collective-permute-done.20 = f32[16,16,128]{2,1,0:T(8,128)S(1)} collective-permute-done((f32[16,16,128]{2,1,0:T(8,128)S(1)}, f32[16,16,128]{2,1,0:T(8,128)S(1)}, u32[]{:S(2)}, u32[]{:S(2)}) %collective-permute-start.20) | collective-permute-done | bytes 131104 | tf_op jit(solution)/shard_map/ppermute | solution.py:26
  459.7 10.8 %fusion.51 = f32[16,16,128]{2,1,0:T(8,128)S(1)} fusion(f32[16,16,128]{2,1,0:T(8,128)S(1)} %collective-permute-done.20, f32[18,18,130]{2,1,0:T(8,128)S(1)} %select_maximum_fusion.18, f32[1,16,128]{2,1,0:T(8,128)S(1)} %collective-permute-done.22, f32[1,16,128]{2,1,0:T(8,128)S(1)} %collective-permute-done.21, f32[16,16,128]{2,1,0:T(8,128)S(1)} %copy-done, ...), kind=kLoop, calls=%fused_computation.153 | loop fusion | flops 1474560 | bytes 1065028 | tf_op jit(solution)/shard_map/add | solution.py:47
  478.2 10.8 %fusion.46 = f32[16,16,128]{2,1,0:T(8,128)S(1)} fusion(f32[16,16,128]{2,1,0:T(8,128)S(1)} %fusion.51, f32[18,18,130]{2,1,0:T(8,128)S(1)} %select_maximum_fusion.16, f32[1,16,128]{2,1,0:T(8,128)S(1)} %collective-permute-done.24, f32[1,16,128]{2,1,0:T(8,128)S(1)} %collective-permute-done.23, f32[16,16,128]{2,1,0:T(8,128)S(1)} %copy-done, f32[]{:T(128)} %fusion.103, ...), kind=kLoop, calls=%fused_computation.142 | loop fusion | flops 1474560 | bytes 1065028 | tf_op jit(solution)/shard_map/add | solution.py:47
  496.2 10.8 %fusion.41 = f32[16,16,128]{2,1,0:T(8,128)S(1)} fusion(f32[16,16,128]{2,1,0:T(8,128)S(1)} %fusion.46, f32[18,18,130]{2,1,0:T(8,128)S(1)} %select_maximum_fusion.14, f32[1,16,128]{2,1,0:T(8,128)S(1)} %collective-permute-done.26, f32[1,16,128]{2,1,0:T(8,128)S(1)} %collective-permute-done.25, f32[16,16,128]{2,1,0:T(8,128)S(1)} %copy-done, f32[]{:T(128)} %fusion.103, ...), kind=kLoop, calls=%fused_computation.131 | loop fusion | flops 1474560 | bytes 1065028 | tf_op jit(solution)/shard_map/add | solution.py:47
  514.1 10.8 %fusion.36 = f32[16,16,128]{2,1,0:T(8,128)S(1)} fusion(f32[16,16,128]{2,1,0:T(8,128)S(1)} %fusion.41, f32[18,18,130]{2,1,0:T(8,128)S(1)} %select_maximum_fusion.12, f32[1,16,128]{2,1,0:T(8,128)S(1)} %collective-permute-done.28, f32[1,16,128]{2,1,0:T(8,128)S(1)} %collective-permute-done.27, f32[16,16,128]{2,1,0:T(8,128)S(1)} %copy-done, f32[]{:T(128)} %fusion.103, ...), kind=kLoop, calls=%fused_computation.120 | loop fusion | flops 1474560 | bytes 1065028 | tf_op jit(solution)/shard_map/add | solution.py:47
  532.0 10.8 %fusion.31 = f32[16,16,128]{2,1,0:T(8,128)S(1)} fusion(f32[16,16,128]{2,1,0:T(8,128)S(1)} %fusion.36, f32[18,18,130]{2,1,0:T(8,128)S(1)} %select_maximum_fusion.10, f32[1,16,128]{2,1,0:T(8,128)S(1)} %collective-permute-done.30, f32[1,16,128]{2,1,0:T(8,128)S(1)} %collective-permute-done.29, f32[16,16,128]{2,1,0:T(8,128)S(1)} %copy-done, f32[]{:T(128)} %fusion.103, ...), kind=kLoop, calls=%fused_computation.109 | loop fusion | flops 1474560 | bytes 1065028 | tf_op jit(solution)/shard_map/add | solution.py:47
  549.9 10.8 %fusion.26 = f32[16,16,128]{2,1,0:T(8,128)S(1)} fusion(f32[16,16,128]{2,1,0:T(8,128)S(1)} %fusion.31, f32[18,18,130]{2,1,0:T(8,128)S(1)} %select_maximum_fusion.8, f32[1,16,128]{2,1,0:T(8,128)S(1)} %collective-permute-done.32, f32[1,16,128]{2,1,0:T(8,128)S(1)} %collective-permute-done.31, f32[16,16,128]{2,1,0:T(8,128)S(1)} %copy-done, f32[]{:T(128)} %fusion.103, ...), kind=kLoop, calls=%fused_computation.98 | loop fusion | flops 1474560 | bytes 1065028 | tf_op jit(solution)/shard_map/add | solution.py:47
  567.9 10.8 %fusion.21 = f32[16,16,128]{2,1,0:T(8,128)S(1)} fusion(f32[16,16,128]{2,1,0:T(8,128)S(1)} %fusion.26, f32[18,18,130]{2,1,0:T(8,128)S(1)} %select_maximum_fusion.6, f32[1,16,128]{2,1,0:T(8,128)S(1)} %collective-permute-done.34, f32[1,16,128]{2,1,0:T(8,128)S(1)} %collective-permute-done.33, f32[16,16,128]{2,1,0:T(8,128)S(1)} %copy-done, f32[]{:T(128)} %fusion.103, ...), kind=kLoop, calls=%fused_computation.87 | loop fusion | flops 1474560 | bytes 1065028 | tf_op jit(solution)/shard_map/add | solution.py:47
  585.8 10.8 %fusion.16 = f32[16,16,128]{2,1,0:T(8,128)S(1)} fusion(f32[16,16,128]{2,1,0:T(8,128)S(1)} %fusion.21, f32[18,18,130]{2,1,0:T(8,128)S(1)} %select_maximum_fusion.4, f32[1,16,128]{2,1,0:T(8,128)S(1)} %collective-permute-done.36, f32[1,16,128]{2,1,0:T(8,128)S(1)} %collective-permute-done.35, f32[16,16,128]{2,1,0:T(8,128)S(1)} %copy-done, f32[]{:T(128)} %fusion.103, ...), kind=kLoop, calls=%fused_computation.76 | loop fusion | flops 1474560 | bytes 1065028 | tf_op jit(solution)/shard_map/add | solution.py:47
  603.7 10.8 %fusion.11 = f32[16,16,128]{2,1,0:T(8,128)S(1)} fusion(f32[16,16,128]{2,1,0:T(8,128)S(1)} %fusion.16, f32[18,18,130]{2,1,0:T(8,128)S(1)} %select_maximum_fusion.2, f32[1,16,128]{2,1,0:T(8,128)S(1)} %collective-permute-done.38, f32[1,16,128]{2,1,0:T(8,128)S(1)} %collective-permute-done.37, f32[16,16,128]{2,1,0:T(8,128)S(1)} %copy-done, f32[]{:T(128)} %fusion.103, ...), kind=kLoop, calls=%fused_computation.65 | loop fusion | flops 1474560 | bytes 1065028 | tf_op jit(solution)/shard_map/add | solution.py:47
  628.8 10.8 %fusion.6 = f32[16,16,128]{2,1,0:T(8,128)S(1)} fusion(f32[16,16,128]{2,1,0:T(8,128)S(1)} %fusion.11, f32[18,18,130]{2,1,0:T(8,128)S(1)} %select_maximum_fusion, f32[1,16,128]{2,1,0:T(8,128)S(1)} %collective-permute-done.40, f32[1,16,128]{2,1,0:T(8,128)S(1)} %collective-permute-done.39, f32[16,16,128]{2,1,0:T(8,128)S(1)} %copy-done, f32[]{:T(128)} %fusion.103, ...), kind=kLoop, calls=%fused_computation.54 | loop fusion | flops 1474560 | bytes 1065028 | tf_op jit(solution)/shard_map/add | solution.py:47
  647.9 215.9 %all-gather.1 = f32[256,4,32]{2,1,0:T(4,128)S(1)} all-gather(f32[4,4,32]{2,1,0:T(4,128)S(1)} %multiply_subtract_fusion), channel_id=3, replica_groups=mesh['tm'=64,'space'=8] {'tm'}, dimensions={0}, use_global_device_ids=true | all-gather | bytes 133120 | tf_op jit(solution)/shard_map/all_gather | solution.py:78
  874.9 11.8 %collective-permute-done.41 = f32[16,16,128]{2,1,0:T(8,128)S(1)} collective-permute-done((f32[16,16,128]{2,1,0:T(8,128)S(1)}, f32[16,16,128]{2,1,0:T(8,128)S(1)}, u32[]{:S(2)}, u32[]{:S(2)}) %collective-permute-start.41) | collective-permute-done | bytes 131104 | tf_op jit(solution)/shard_map/ppermute | solution.py:26
  (154 shorter events, 199.6 us)
Async XLA Ops:
  0.8 9.4 %collective-permute-start.1 = (f32[1,16,128]{2,1,0:T(8,128)S(1)}, f32[1,16,128]{2,1,0:T(8,128)S(1)}, u32[]{:S(2)}, u32[]{:S(2)}) collective-permute-start(f32[1,16,128]{2,1,0:T(8,128)S(1)} %get-tuple-element.43), channel_id=1, source_target_pairs={{0,1},{1,2},{2,3},{3,4},{4,5},{5,6},{6,7},{8,9},{9,10},{10,11},{11... | collective-permute-start | bytes 24584 | tf_op jit(solution)/shard_map/ppermute | solution.py:15
  2.7 7.5 collective-permute-start
  23.3 6.6 collective-permute-start.3
  43.2 5.6 collective-permute-start.5
  61.1 6.0 collective-permute-start.7
  79.5 5.7 collective-permute-start.9
  97.5 5.6 collective-permute-start.11
  115.5 5.6 collective-permute-start.13
  133.4 5.6 collective-permute-start.15
  151.3 5.6 collective-permute-start.17
  169.2 13.9 %collective-permute-start.19 = (f32[1,16,128]{2,1,0:T(8,128)S(1)}, f32[1,16,128]{2,1,0:T(8,128)S(1)}, u32[]{:S(2)}, u32[]{:S(2)}) collective-permute-start(f32[1,16,128]{2,1,0:T(8,128)S(1)} %get-tuple-element.25), channel_id=1, source_target_pairs={{0,1},{1,2},{2,3},{3,4},{4,5},{5,6},{6,7},{8,9},{9,10},{10,11},{11... | collective-permute-start | bytes 24584 | tf_op jit(solution)/shard_map/ppermute | solution.py:15
  172.9 10.3 %collective-permute-start.18 = (f32[1,16,128]{2,1,0:T(8,128)S(1)}, f32[1,16,128]{2,1,0:T(8,128)S(1)}, u32[]{:S(2)}, u32[]{:S(2)}) collective-permute-start(f32[1,16,128]{2,1,0:T(8,128)S(1)} %get-tuple-element.26), channel_id=1, source_target_pairs={{1,0},{2,1},{3,2},{4,3},{5,4},{6,5},{7,6},{9,8},{10,9},{11,10},{12... | collective-permute-start | bytes 24584 | tf_op jit(solution)/shard_map/ppermute | solution.py:18
  437.6 15.0 %collective-permute-start.20 = (f32[16,16,128]{2,1,0:T(8,128)S(1)}, f32[16,16,128]{2,1,0:T(8,128)S(1)}, u32[]{:S(2)}, u32[]{:S(2)}) collective-permute-start(f32[16,16,128]{2,1,0:T(8,128)S(1)} %add.550), channel_id=1, source_target_pairs={{504,0},{0,8},{8,16},{16,24},{24,32},{32,40},{40,48},{48,56},{56,6... | collective-permute-start | bytes 393224 | tf_op jit(solution)/shard_map/ppermute | solution.py:26
  470.5 6.2 collective-permute-start.24
  489.1 5.6 collective-permute-start.26
  507.0 5.6 collective-permute-start.28
  524.9 5.6 collective-permute-start.30
  542.8 5.6 collective-permute-start.32
  560.8 5.6 collective-permute-start.34
  578.7 5.6 collective-permute-start.36
  596.6 5.6 collective-permute-start.38
  614.5 14.1 %collective-permute-start.40 = (f32[1,16,128]{2,1,0:T(8,128)S(1)}, f32[1,16,128]{2,1,0:T(8,128)S(1)}, u32[]{:S(2)}, u32[]{:S(2)}) collective-permute-start(f32[1,16,128]{2,1,0:T(8,128)S(1)} %get-tuple-element.5), channel_id=1, source_target_pairs={{0,1},{1,2},{2,3},{3,4},{4,5},{5,6},{6,7},{8,9},{9,10},{10,11},{11... | collective-permute-start | bytes 24584 | tf_op jit(solution)/shard_map/ppermute | solution.py:15
  618.2 10.5 %collective-permute-start.39 = (f32[1,16,128]{2,1,0:T(8,128)S(1)}, f32[1,16,128]{2,1,0:T(8,128)S(1)}, u32[]{:S(2)}, u32[]{:S(2)}) collective-permute-start(f32[1,16,128]{2,1,0:T(8,128)S(1)} %get-tuple-element.6), channel_id=1, source_target_pairs={{1,0},{2,1},{3,2},{4,3},{5,4},{6,5},{7,6},{9,8},{10,9},{11,10},{12... | collective-permute-start | bytes 24584 | tf_op jit(solution)/shard_map/ppermute | solution.py:18
  871.7 15.0 %collective-permute-start.41 = (f32[16,16,128]{2,1,0:T(8,128)S(1)}, f32[16,16,128]{2,1,0:T(8,128)S(1)}, u32[]{:S(2)}, u32[]{:S(2)}) collective-permute-start(f32[16,16,128]{2,1,0:T(8,128)S(1)} %add.621), channel_id=1, source_target_pairs={{504,0},{0,8},{8,16},{16,24},{24,32},{32,40},{40,48},{48,56},{56,6... | collective-permute-start | bytes 393224 | tf_op jit(solution)/shard_map/ppermute | solution.py:26
  (22 other events, 266.0 us)
where the time goes:
time: 892 us; the launch traced here: 887 us
  blocking collectives  443 us (50%)
  other arithmetic  235 us (26%)
  starting transfers between devices  119 us (13%)
  waiting for transfers between devices  47.6 us (5%)
  local copies, waits for them, and re-layouts  41.1 us (5%)
    all_gather x2, blocking collectives, body(): pieces = lax.all_gather(jump_now[None], 'tm', axis=0, tiled=True)  443 us
    add x20, other arithmetic, slab_update(): return field_now + cell_coef * (neighbours - 6.0 * field_now) + forcing  218 us
    ppermute x20, starting transfers between devices, padded_2(): lax.ppermute(lax.slice_in_dim(block, block.shape[dim] - width, None, axis...  69.2 us
    ppermute x20, starting transfers between devices, padded_2(): lax.ppermute(lax.slice_in_dim(block, 0, width, axis=dim), axis, backward)  44.5 us
    ppermute x2, waiting for transfers between devices, from_behind(): return lax.ppermute(block, axis, route)  24.9 us
    ppermute x20, waiting for transfers between devices, padded_2(): lax.ppermute(lax.slice_in_dim(block, 0, width, axis=dim), axis, backward)  22.7 us
  transfers between devices with their start and end apart: 42, of which 19 were waited for; matrix products, arithmetic and copies ran while one was open for 2% of the time, Pallas kernels for 0%

commit v1 on v0

v1 whole, which is shorter than its diff:
```python
import jax
import jax.numpy as jnp
from jax import lax
from jax.experimental import pallas as pl
from jax.experimental.pallas import tpu as pltpu
from jax.sharding import PartitionSpec as P

FINE = 10
WINDOWS = 64
SLABS = 8
LAYERS = 16
HALO = FINE
EXT = LAYERS + 2 * HALO
MESH = pl.DeviceIdType.MESH
GROUPS = ((1, 3), (4, 3), (7, 4))


def roll(x, shift, axis):
    return pltpu.roll(x, shift % x.shape[axis], axis)


def make_kernel():
    def kernel(
        start, material, source, cond, amp, phase, rate, out,
        nat_u, nat_m, nat_s, u, coef, force, src, level, jbuf, kbuf, ksend,
        weight, cown, cghost, dhalo, fin,
        loc_sem, h_send, h_recv, j_send, j_recv, k_send, k_recv,
        d_send, d_recv, c_send, c_recv, l_send, l_recv, f_send, f_recv,
    ):
        tm = lax.axis_index("tm")
        slab = lax.axis_index("space")
        yy = lax.rem(tm, 8)
        group = tm // 8
        xx = lax.rem(group, 4)
        zz = group // 4
        has_low = slab > 0
        has_high = slab < SLABS - 1

        def y_peer(j):
            return (group * 8 + lax.rem(yy + j, 8), slab)

        def g_index(dz, dx):
            return lax.rem(zz + dz, 2) * 4 + lax.rem(xx + dx, 4)

        def g_peer(dz, dx):
            return (g_index(dz, dx) * 8 + yy, slab)

        def t_peer(shift):
            return (lax.rem(tm + shift + WINDOWS, WINDOWS), slab)

        own = pl.ds(HALO, LAYERS)
        locals_ = [
            pltpu.make_async_copy(start.at[0], nat_u.at[own], loc_sem.at[0]),
            pltpu.make_async_copy(material, nat_m.at[own], loc_sem.at[1]),
            pltpu.make_async_copy(source, nat_s.at[own], loc_sem.at[2]),
        ]
        for copy in locals_:
            copy.start()

        barrier = pltpu.get_barrier_semaphore()

        def greet(peer):
            pl.semaphore_signal(barrier, inc=1, device_id=peer, device_id_type=MESH)

        @pl.when(has_low)
        def _():
            greet((tm, slab - 1))

        @pl.when(has_high)
        def _():
            greet((tm, slab + 1))

        for j in range(1, 8):
            greet(y_peer(j))
        pairs = [(dz, dx) for dz in (1, 0) for dx in (2, 1, 3, 0) if (dz, dx) != (0, 0)]
        for dz, dx in pairs:
            greet(g_peer(dz, dx))
        for shift in (1, -1, 2, -2):
            greet(t_peer(shift))

        level_own = amp[phase[0]]
        level[0] = jnp.full((8, 128), level_own, jnp.float32)

        sides = jnp.where(has_low, 1, 0) + jnp.where(has_high, 1, 0)
        pl.semaphore_wait(barrier, 18 + sides)

        def halo_copies(side):
            peer = (tm, slab - 1) if side == 0 else (tm, slab + 1)
            rows = pl.ds(0, HALO) if side == 0 else pl.ds(LAYERS - HALO, HALO)
            ghost = pl.ds(HALO + LAYERS, HALO) if side == 0 else pl.ds(0, HALO)
            sources = (start.at[0, rows], material.at[rows], source.at[rows])
            targets = (nat_u.at[ghost], nat_m.at[ghost], nat_s.at[ghost])
            return [
                pltpu.make_async_remote_copy(
                    src_ref=a, dst_ref=b, send_sem=h_send.at[side, i],
                    recv_sem=h_recv.at[side, i], device_id=peer, device_id_type=MESH,
                )
                for i, (a, b) in enumerate(zip(sources, targets))
            ]

        @pl.when(has_high)
        def _():
            for copy in halo_copies(1):
                copy.start()

        @pl.when(has_low)
        def _():
            for copy in halo_copies(0):
                copy.start()

        level_copy = pltpu.make_async_remote_copy(
            src_ref=level.at[0], dst_ref=level.at[1], send_sem=l_send,
            recv_sem=l_recv, device_id=t_peer(-1), device_id_type=MESH,
        )
        level_copy.start()

        sub = lax.broadcasted_iota(jnp.int32, (8, 128), 0)
        lane = lax.broadcasted_iota(jnp.int32, (8, 128), 1)
        first_lane, last_lane = lane == 0, lane == 127
        first_sub, last_sub = sub == 0, sub == 7
        even_sub, even_lane = (sub & 1) == 0, (lane & 1) == 0
        low_pair = (lane & 3) < 2
        owner = (sub >> 1) == (lane & 3)
        pick = sub == 2 * (lane & 3)
        zero = jnp.zeros((8, 128), jnp.float32)

        def lane_total(x):
            x = x + jnp.where(even_lane, roll(x, -1, 1), roll(x, 1, 1))
            return x + jnp.where(low_pair, roll(x, -2, 1), roll(x, 2, 1))

        def block_mean(layers):
            total = layers[0]
            for part in layers[1:]:
                total = total + part
            total = total + jnp.where(even_sub, roll(total, -1, 0), roll(total, 1, 0))
            return lane_total(total) * (1.0 / 64.0)

        def pack(means):
            rows = [
                jnp.sum(jnp.where(pick, m, zero), axis=0, keepdims=True) for m in means
            ]
            return jnp.concatenate(rows, axis=0)

        def unpack(row):
            wide = jnp.broadcast_to(row, (8, 128))
            return lane_total(jnp.where(owner, wide, zero))

        def clear(side):
            def go(i, _):
                k = i + (HALO + LAYERS if side else 0)
                nat_u[k] = jnp.zeros((16, 128), jnp.float32)
                nat_s[k] = jnp.zeros((16, 128), jnp.float32)
                nat_m[k] = jnp.zeros((16, 128), jnp.int32)
                dhalo[side, i] = jnp.zeros((2, 8, 128), jnp.float32)
                return 0

            lax.fori_loop(0, HALO, go, 0)
            cghost[side] = jnp.zeros((4, 128), jnp.float32)

        @pl.when(jnp.logical_not(has_low))
        def _():
            clear(0)

        @pl.when(jnp.logical_not(has_high))
        def _():
            clear(1)

        spread_row = lax.broadcasted_iota(jnp.int32, (32, 128), 0)
        spread_col = lax.broadcasted_iota(jnp.int32, (32, 128), 1)
        spread = jnp.where(spread_row == (spread_col >> 2), 1.0, 0.0).astype(jnp.float32)
        quarter = lax.broadcasted_iota(jnp.int32, (4, 128), 0) == (
            lax.broadcasted_iota(jnp.int32, (4, 128), 1) & 3
        )
        rows = []
        for zc in range(4):
            wide = jnp.dot(
                rate[zc], spread, precision=lax.Precision.HIGHEST,
                preferred_element_type=jnp.float32,
            )
            rows.append(jnp.sum(jnp.where(quarter, wide, 0.0), axis=0, keepdims=True))
        packed_rate = jnp.concatenate(rows, axis=0)
        step_rate = packed_rate * (-1.0 / WINDOWS)
        decay = jnp.exp(step_rate)
        unclose = 1.0 / (1.0 - jnp.exp(-packed_rate))

        def powers(i, _):
            weight[i] = jnp.exp(step_rate * i.astype(jnp.float32))
            return 0

        lax.fori_loop(0, WINDOWS, powers, 0)

        def lookup(m):
            picks = [cond[i] for i in range(16)]
            for bit in range(4):
                on = (m & (1 << bit)) != 0
                picks = [
                    jnp.where(on, picks[2 * i + 1], picks[2 * i])
                    for i in range(len(picks) // 2)
                ]
            return picks[0]

        level1 = level[0]

        def arrange(lo, count, gain):
            def go(i, _):
                for half in range(2):
                    rows = pl.ds(half, 8, stride=2)
                    k = lo + i
                    u[k, half] = nat_u[k, rows, :]
                    c = lookup(nat_m[k, rows, :])
                    coef[k, half] = c if gain is None else c * gain
                    s = nat_s[k, rows, :]
                    src[k, half] = s
                    force[k, half] = level1 * s
                return 0

            lax.fori_loop(0, count, go, 0, unroll=2)

        for copy in locals_:
            copy.wait()
        arrange(HALO, LAYERS, None)

        def slab_means():
            means = []
            for zc in range(4):
                base = HALO + 4 * zc
                means.append(
                    block_mean([u[base + i, half] for i in range(4) for half in range(2)])
                )
            return means

        start_mean = pack(slab_means())

        @pl.when(has_low)
        def _():
            for copy in halo_copies(1):
                copy.wait_recv()

        @pl.when(has_high)
        def _():
            for copy in halo_copies(0):
                copy.wait_recv()

        arrange(0, HALO, jnp.where(has_low, 1.0, 0.0))
        arrange(HALO + LAYERS, HALO, jnp.where(has_high, 1.0, 0.0))

        def sweep(lo, hi):
            before = (u[lo - 1, 0], u[lo - 1, 1])
            here = (u[lo, 0], u[lo, 1])
            for k in range(lo, hi):
                after = (u[k + 1, 0], u[k + 1, 1])
                even, odd = here
                across = (
                    odd + jnp.where(first_sub, zero, roll(odd, 1, 0)),
                    even + jnp.where(last_sub, zero, roll(even, -1, 0)),
                )
                for half in range(2):
                    now = here[half]
                    total = before[half] + after[half] + across[half]
                    total = total + jnp.where(first_lane, zero, roll(now, 1, 1))
                    total = total + jnp.where(last_lane, zero, roll(now, -1, 1))
                    u[k, half] = now + coef[k, half] * (total - 6.0 * now) + force[k, half]
                before, here = here, after

        def fine():
            for first, count in GROUPS:
                def go(i, _):
                    sweep(first, EXT - first)
                    return 0

                lax.fori_loop(0, count, go, 0)

        def coarse_solve(it, jump, offset, between):
            jbuf[it, 0] = jump
            sends = []
            for j in (4, 3, 5, 2, 6, 1, 7):
                copy = pltpu.make_async_remote_copy(
                    src_ref=jbuf.at[it, 0], dst_ref=jbuf.at[it, j],
                    send_sem=j_send.at[it, j], recv_sem=j_recv.at[it, j],
                    device_id=y_peer(j), device_id_type=MESH,
                )
                copy.start()
                sends.append(copy)
            between()
            for copy in sends:
                copy.wait_recv()
            jumps = [jbuf[it, j] for j in range(8)]

            def partial(target_group):
                total = None
                for j in range(8):
                    origin = group * 8 + lax.rem(yy - j + 8, 8)
                    lag = lax.rem(target_group * 8 + yy - offset - origin + 2 * WINDOWS, WINDOWS)
                    term = weight[lag] * jumps[j]
                    total = term if total is None else total + term
                return total

            for dz, dx in pairs:
                slot = dz * 4 + dx
                ksend[it, slot] = partial(g_index(dz, dx))
                copy = pltpu.make_async_remote_copy(
                    src_ref=ksend.at[it, slot], dst_ref=kbuf.at[it, slot],
                    send_sem=k_send.at[it, slot], recv_sem=k_recv.at[it, slot],
                    device_id=g_peer(dz, dx), device_id_type=MESH,
                )
                copy.start()
                sends.append(copy)
            total = partial(group)
            for copy in sends[7:]:
                copy.wait_recv()
            for dz, dx in pairs:
                total = total + kbuf[it, dz * 4 + dx]
            return total * unclose, sends

        pending = []
        fine()

        def detach():
            means = slab_means()
            for zc in range(4):
                for i in range(4):
                    k = HALO + 4 * zc + i
                    for half in range(2):
                        u[k, half] = u[k, half] - means[zc]
            return pack(means)

        end_mean = detach()
        jump = end_mean - decay * start_mean

        def halo2(side):
            peer = (tm, slab - 1) if side == 0 else (tm, slab + 1)
            rows = pl.ds(HALO, HALO) if side == 0 else pl.ds(LAYERS, HALO)
            return pltpu.make_async_remote_copy(
                src_ref=u.at[rows], dst_ref=dhalo.at[1 - side],
                send_sem=d_send.at[side], recv_sem=d_recv.at[side],
                device_id=peer, device_id_type=MESH,
            )

        def ghost_mean(side):
            peer = (tm, slab - 1) if side == 0 else (tm, slab + 1)
            return pltpu.make_async_remote_copy(
                src_ref=cown, dst_ref=cghost.at[1 - side],
                send_sem=c_send.at[side], recv_sem=c_recv.at[side],
                device_id=peer, device_id_type=MESH,
            )

        def between1():
            @pl.when(has_high)
            def _():
                halo2(1).start()

            @pl.when(has_low)
            def _():
                halo2(0).start()

            level_copy.wait_recv()
            level2 = level[1]

            def go(k, _):
                for half in range(2):
                    force[k, half] = level2 * src[k, half]
                return 0

            lax.fori_loop(0, EXT, go, 0, unroll=4)

        coarse, sends = coarse_solve(0, jump, 0, between1)
        pending += sends
        cown[...] = coarse

        @pl.when(has_high)
        def _():
            ghost_mean(1).start()
            halo2(1).wait_send()

        @pl.when(has_low)
        def _():
            ghost_mean(0).start()
            halo2(0).wait_send()

        for zc in range(4):
            wide = unpack(coarse[zc:zc + 1])
            for i in range(4):
                k = HALO + 4 * zc + i
                for half in range(2):
                    u[k, half] = u[k, half] + wide

        @pl.when(has_low)
        def _():
            halo2(1).wait_recv()
            ghost_mean(1).wait_recv()

        @pl.when(has_high)
        def _():
            halo2(0).wait_recv()
            ghost_mean(0).wait_recv()

        low_wide = {r: unpack(cghost[0, r:r + 1, :]) for r in (1, 2, 3)}
        high_wide = {r: unpack(cghost[1, r:r + 1, :]) for r in (0, 1, 2)}
        for i in range(HALO):
            for half in range(2):
                u[i, half] = dhalo[0, i, half] + low_wide[(LAYERS - HALO + i) // 4]
                u[HALO + LAYERS + i, half] = dhalo[1, i, half] + high_wide[i // 4]

        fine()

        end_mean = detach()
        jump = end_mean - decay * coarse
        final_copy = pltpu.make_async_remote_copy(
            src_ref=u.at[own], dst_ref=fin, send_sem=f_send, recv_sem=f_recv,
            device_id=t_peer(2), device_id_type=MESH,
        )
        coarse, sends = coarse_solve(1, jump, 2, final_copy.start)
        pending += sends
        wides = [unpack(coarse[zc:zc + 1]) for zc in range(4)]
        final_copy.wait_recv()
        for zc in range(4):
            for i in range(4):
                k = 4 * zc + i
                for half in range(2):
                    out[0, k, pl.ds(half, 8, stride=2), :] = fin[k, half] + wides[zc]

        for copy in pending:
            copy.wait_send()
        final_copy.wait_send()
        level_copy.wait_send()

        @pl.when(has_high)
        def _():
            for copy in halo_copies(1):
                copy.wait_send()
            ghost_mean(1).wait_send()

        @pl.when(has_low)
        def _():
            for copy in halo_copies(0):
                copy.wait_send()
            ghost_mean(0).wait_send()

    return kernel


def body(start_states, material, source, conductivity, tide_amp, phase, coarse_rate):
    f32 = jnp.float32
    smem = pl.BlockSpec(memory_space=pltpu.SMEM)
    hbm = pl.BlockSpec(memory_space=pl.ANY)
    vmem = pl.BlockSpec(memory_space=pltpu.VMEM)
    dma = pltpu.SemaphoreType.DMA
    field = pltpu.VMEM((EXT, 2, 8, 128), f32)
    return pl.pallas_call(
        make_kernel(),
        out_shape=jax.ShapeDtypeStruct((1, LAYERS, 16, 128), f32),
        in_specs=[hbm, hbm, hbm, smem, smem, smem, vmem],
        out_specs=vmem,
        scratch_shapes=[
            pltpu.VMEM((EXT, 16, 128), f32),
            pltpu.VMEM((EXT, 16, 128), jnp.int32),
            pltpu.VMEM((EXT, 16, 128), f32),
            field, field, field, field,
            pltpu.VMEM((2, 8, 128), f32),
            pltpu.VMEM((2, 8, 4, 128), f32),
            pltpu.VMEM((2, 8, 4, 128), f32),
            pltpu.VMEM((2, 8, 4, 128), f32),
            pltpu.VMEM((WINDOWS, 4, 128), f32),
            pltpu.VMEM((4, 128), f32),
            pltpu.VMEM((2, 4, 128), f32),
            pltpu.VMEM((2, HALO, 2, 8, 128), f32),
            pltpu.VMEM((LAYERS, 2, 8, 128), f32),
            dma((3,)), dma((2, 3)), dma((2, 3)),
            dma((2, 8)), dma((2, 8)), dma((2, 8)), dma((2, 8)),
            dma((2,)), dma((2,)), dma((2,)), dma((2,)),
            dma(()), dma(()), dma(()), dma(()),
        ],
        compiler_params=pltpu.CompilerParams(collective_id=0, has_side_effects=True),
    )(start_states, material, source, conductivity, tide_amp, phase, coarse_rate)


def solution(mesh):
    placed = (
        P("tm", "space", None, None),
        P("space", None, None),
        P("space", None, None),
        P(),
        P(),
        P("tm"),
        P("space", None, None),
    )
    return jax.shard_map(
        body, mesh=mesh, in_specs=placed, out_specs=P("tm", "space", None, None), check_vma=False
    )
```

time: 892 us -> 53.1 us (0.06)
  the two profiles are of different devices: /device:TPU:64 before, /device:TPU:1 now
where the time goes in v1:
time: 53.1 us; the launch traced here: 52.9 us
  Pallas kernels  50.7 us (95%)
  local copies, waits for them, and re-layouts  1.57 us (3%)
  between operations  0.66 us (1%)
    pallas_call x1, Pallas kernels, body(): pl.pallas_call(make_kernel(), out_shape=jax.ShapeDtypeStruct((1, LAYERS,...  50.7 us
    unnamed x1, local copies, waits for them, and re-layouts  1.57 us

profile of v1, /device:TPU:1, one launch (start us, length us, event | category | flops | bytes accessed | tf_op | source)
XLA Modules:
  0.0 52.9 jit_solution(4408213029828464389)
XLA Ops:
  0.7 50.7 %shard_map.73 = f32[1,16,16,128]{3,2,1,0:T(8,128)} custom-call(f32[1,16,16,128]{3,2,1,0:T(8,128)} %start.1, s32[16,16,128]{2,1,0:T(8,128)} %material.1, f32[16,16,128]{2,1,0:T(8,128)} %source.1, f32[16]{0:T(128)} %cond.1, f32[12]{0:T(128)} %amp.1, s32[1]{0:T(128)S(6)} %copy.9.phase, f32[4,4,32]{2,1,0:T(4,128)} %rate.1), custom_call_target="tpu_custom_call" | custom-call | tf_op jit(solution)/shard_map/pallas_call | solution.py:449
  51.4 1.6 %copy.10 = f32[1,16,16,128]{3,2,1,0:T(8,128)} copy(f32[1,16,16,128]{3,2,1,0:T(8,128)} %shard_map.73) | data formatting | bytes 262144

commit v2 on v1

--- a/solution.py
+++ b/solution.py
@@ -22,10 +22,10 @@
 def make_kernel():
     def kernel(
         start, material, source, cond, amp, phase, rate, out,
-        nat_u, nat_m, nat_s, u, coef, force, src, level, jbuf, kbuf, ksend,
-        weight, cown, cghost, dhalo, fin,
+        nat_u, nat_m, nat_s, u, coef, force, src, jbuf, ksend, kbuf, tsend,
+        ghost, weight, dhalo, fin,
         loc_sem, h_send, h_recv, j_send, j_recv, k_send, k_recv,
-        d_send, d_recv, c_send, c_recv, l_send, l_recv, f_send, f_recv,
+        d_send, d_recv, g_send, g_recv, f_send, f_recv, near, ring, cross, up,
     ):
         tm = lax.axis_index("tm")
         slab = lax.axis_index("space")
@@ -36,17 +36,13 @@
         has_low = slab > 0
         has_high = slab < SLABS - 1
 
-        def y_peer(j):
-            return (group * 8 + lax.rem(yy + j, 8), slab)
-
-        def g_index(dz, dx):
-            return lax.rem(zz + dz, 2) * 4 + lax.rem(xx + dx, 4)
-
-        def g_peer(dz, dx):
-            return (g_index(dz, dx) * 8 + yy, slab)
-
-        def t_peer(shift):
-            return (lax.rem(tm + shift + WINDOWS, WINDOWS), slab)
+        def plane_peer(dx, dy):
+            x, y = lax.rem(xx + dx, 4), lax.rem(yy + dy, 8)
+            return ((zz * 4 + x) * 8 + y, slab)
+
+        twin_tm = lax.rem(tm + 32, WINDOWS)
+        twin = (twin_tm, slab)
+        last = lax.rem(tm + 2, WINDOWS)
 
         own = pl.ds(HALO, LAYERS)
         locals_ = [
@@ -70,19 +66,22 @@
         def _():
             greet((tm, slab + 1))
 
-        for j in range(1, 8):
-            greet(y_peer(j))
-        pairs = [(dz, dx) for dz in (1, 0) for dx in (2, 1, 3, 0) if (dz, dx) != (0, 0)]
-        for dz, dx in pairs:
-            greet(g_peer(dz, dx))
-        for shift in (1, -1, 2, -2):
-            greet(t_peer(shift))
+        for dx, dy in ((0, 1), (0, 7), (1, 0), (3, 0)):
+            greet(plane_peer(dx, dy))
+
+        @pl.when(zz == 0)
+        def _():
+            greet(twin)
+
+        def tell(sem, peers):
+            for peer in peers:
+                pl.semaphore_signal(sem, inc=1, device_id=peer, device_id_type=MESH)
 
         level_own = amp[phase[0]]
-        level[0] = jnp.full((8, 128), level_own, jnp.float32)
+        jbuf[0, 0, 4:8, :] = jnp.full((4, 128), level_own, jnp.float32)
 
         sides = jnp.where(has_low, 1, 0) + jnp.where(has_high, 1, 0)
-        pl.semaphore_wait(barrier, 18 + sides)
+        pl.semaphore_wait(barrier, 4 + sides + zz)
 
         def halo_copies(side):
             peer = (tm, slab - 1) if side == 0 else (tm, slab + 1)
@@ -108,11 +107,12 @@
             for copy in halo_copies(0):
                 copy.start()
 
-        level_copy = pltpu.make_async_remote_copy(
-            src_ref=level.at[0], dst_ref=level.at[1], send_sem=l_send,
-            recv_sem=l_recv, device_id=t_peer(-1), device_id_type=MESH,
-        )
-        level_copy.start()
+        @pl.when(zz == 1)
+        def _():
+            tell(up, (twin,))
+
+        around = tuple(plane_peer(dx, dy) for dx, dy in ((0, 1), (0, 7), (1, 0), (3, 0)))
+        tell(near, around)
 
         sub = lax.broadcasted_iota(jnp.int32, (8, 128), 0)
         lane = lax.broadcasted_iota(jnp.int32, (8, 128), 1)
@@ -155,7 +155,8 @@
                 return 0
 
             lax.fori_loop(0, HALO, go, 0)
-            cghost[side] = jnp.zeros((4, 128), jnp.float32)
+            for part in range(2):
+                ghost[part, side] = jnp.zeros((4, 128), jnp.float32)
 
         @pl.when(jnp.logical_not(has_low))
         def _():
@@ -183,11 +184,18 @@
         decay = jnp.exp(step_rate)
         unclose = 1.0 / (1.0 - jnp.exp(-packed_rate))
 
-        def powers(i, _):
-            weight[i] = jnp.exp(step_rate * i.astype(jnp.float32))
-            return 0
-
-        lax.fori_loop(0, WINDOWS, powers, 0)
+        def powers(it):
+            def go(i, _):
+                dx, dy = i // 8, lax.rem(i, 8)
+                lag = (xx - lax.rem(xx - dx + 4, 4)) * 8 + yy - lax.rem(yy - dy + 8, 8)
+                for half in range(2):
+                    power = lax.rem(lag - 2 * it + 32 * half + 2 * WINDOWS, WINDOWS)
+                    weight[it, half, i] = jnp.exp(step_rate * power.astype(jnp.float32)) * unclose
+                return 0
+
+            lax.fori_loop(0, 32, go, 0, unroll=2)
+
+        powers(0)
 
         def lookup(m):
             picks = [cond[i] for i in range(16)]
@@ -199,7 +207,7 @@
                 ]
             return picks[0]
 
-        level1 = level[0]
+        level1 = level_own
 
         def arrange(lo, count, gain):
             def go(i, _):
@@ -216,6 +224,8 @@
 
             lax.fori_loop(0, count, go, 0, unroll=2)
 
+        pl.semaphore_wait(near, 4)
+        tell(ring, tuple(plane_peer(dx, dy) for dx, dy in ((0, 2), (0, 6), (1, 0), (3, 0))))
         for copy in locals_:
             copy.wait()
         arrange(HALO, LAYERS, None)
@@ -270,48 +280,70 @@
 
                 lax.fori_loop(0, count, go, 0)
 
-        def coarse_solve(it, jump, offset, between):
-            jbuf[it, 0] = jump
+        def coarse_solve(it, jump, between):
+            rows = pl.ds(0, 8 if it == 0 else 4)
+            jbuf[it, 0, 0:4, :] = jump
             sends = []
-            for j in (4, 3, 5, 2, 6, 1, 7):
+            for dx, dy in peers:
+                slot = 8 * dx + dy
                 copy = pltpu.make_async_remote_copy(
-                    src_ref=jbuf.at[it, 0], dst_ref=jbuf.at[it, j],
-                    send_sem=j_send.at[it, j], recv_sem=j_recv.at[it, j],
-                    device_id=y_peer(j), device_id_type=MESH,
+                    src_ref=jbuf.at[it, 0, rows], dst_ref=jbuf.at[it, slot, rows],
+                    send_sem=j_send.at[it, slot], recv_sem=j_recv.at[it, slot],
+                    device_id=plane_peer(dx, dy), device_id_type=MESH,
                 )
                 copy.start()
                 sends.append(copy)
             between()
             for copy in sends:
                 copy.wait_recv()
-            jumps = [jbuf[it, j] for j in range(8)]
-
-            def partial(target_group):
-                total = None
-                for j in range(8):
-                    origin = group * 8 + lax.rem(yy - j + 8, 8)
-                    lag = lax.rem(target_group * 8 + yy - offset - origin + 2 * WINDOWS, WINDOWS)
-                    term = weight[lag] * jumps[j]
-                    total = term if total is None else total + term
-                return total
-
-            for dz, dx in pairs:
-                slot = dz * 4 + dx
-                ksend[it, slot] = partial(g_index(dz, dx))
-                copy = pltpu.make_async_remote_copy(
-                    src_ref=ksend.at[it, slot], dst_ref=kbuf.at[it, slot],
-                    send_sem=k_send.at[it, slot], recv_sem=k_recv.at[it, slot],
-                    device_id=g_peer(dz, dx), device_id_type=MESH,
-                )
-                copy.start()
-                sends.append(copy)
-            total = partial(group)
-            for copy in sends[7:]:
-                copy.wait_recv()
-            for dz, dx in pairs:
-                total = total + kbuf[it, dz * 4 + dx]
-            return total * unclose, sends
-
+
+            def weigh(half):
+                terms = [weight[it, half, i] * jbuf[it, i, 0:4, :] for i in range(32)]
+                while len(terms) > 1:
+                    terms = [a + b for a, b in zip(terms[::2], terms[1::2])]
+                return terms[0]
+
+            ksend[it, 0:4, :] = weigh(1)
+            if it == 0:
+                ksend[0, 4:8, :] = jbuf[0, 31, 4:8, :]
+            copy = pltpu.make_async_remote_copy(
+                src_ref=ksend.at[it, rows], dst_ref=kbuf.at[it, rows],
+                send_sem=k_send.at[it], recv_sem=k_recv.at[it],
+                device_id=twin, device_id_type=MESH,
+            )
+            copy.start()
+            sends.append(copy)
+            if it == 0:
+                ghost_step(0)
+            total = weigh(0)
+            if it == 0:
+                tsend[...] = total
+                ghost_step(1)
+            copy.wait_recv()
+            return total + kbuf[it, 0:4, :], sends
+
+        def ghost_copy(part, side):
+            target = (twin_tm if part == 0 else tm, slab - 1 if side == 0 else slab + 1)
+            return pltpu.make_async_remote_copy(
+                src_ref=ksend.at[0, pl.ds(0, 4)] if part == 0 else tsend,
+                dst_ref=ghost.at[part, 1 - side],
+                send_sem=g_send.at[part, side], recv_sem=g_recv.at[part, 1 - side],
+                device_id=target, device_id_type=MESH,
+            )
+
+        def ghost_step(part):
+            @pl.when(has_high)
+            def _():
+                ghost_copy(part, 1).start()
+
+            @pl.when(has_low)
+            def _():
+                ghost_copy(part, 0).start()
+
+        peers = sorted(
+            [(dx, dy) for dx in range(4) for dy in range(8) if dx + dy > 0],
+            key=lambda p: -min(p[0], 4 - p[0]) - min(p[1], 8 - p[1]),
+        )
         pending = []
         fine()
 
@@ -336,14 +368,6 @@
                 device_id=peer, device_id_type=MESH,
             )
 
-        def ghost_mean(side):
-            peer = (tm, slab - 1) if side == 0 else (tm, slab + 1)
-            return pltpu.make_async_remote_copy(
-                src_ref=cown, dst_ref=cghost.at[1 - side],
-                send_sem=c_send.at[side], recv_sem=c_recv.at[side],
-                device_id=peer, device_id_type=MESH,
-            )
-
         def between1():
             @pl.when(has_high)
             def _():
@@ -353,28 +377,30 @@
             def _():
                 halo2(0).start()
 
-            level_copy.wait_recv()
-            level2 = level[1]
-
-            def go(k, _):
-                for half in range(2):
-                    force[k, half] = level2 * src[k, half]
-                return 0
-
-            lax.fori_loop(0, EXT, go, 0, unroll=4)
-
-        coarse, sends = coarse_solve(0, jump, 0, between1)
+            powers(1)
+
+            @pl.when(zz == 1)
+            def _():
+                pl.semaphore_wait(up, 1)
+
+        pl.semaphore_wait(ring, 4)
+        tell(cross, (plane_peer(0, 2), plane_peer(0, 6)))
+
+        @pl.when(zz == 0)
+        def _():
+            pl.semaphore_wait(up, 1)
+            tell(up, (twin,))
+
+        pl.semaphore_wait(cross, 2)
+        coarse, sends = coarse_solve(0, jump, between1)
         pending += sends
-        cown[...] = coarse
 
         @pl.when(has_high)
         def _():
-            ghost_mean(1).start()
             halo2(1).wait_send()
 
         @pl.when(has_low)
         def _():
-            ghost_mean(0).start()
             halo2(0).wait_send()
 
         for zc in range(4):
@@ -384,18 +410,33 @@
                 for half in range(2):
                     u[k, half] = u[k, half] + wide
 
+        level2 = jnp.where(
+            yy < 7, jbuf[0, 7, 4:5, :],
+            jnp.where(xx < 3, jbuf[0, 31, 4:5, :], kbuf[0, 4:5, :]),
+        )
+        level2 = jnp.broadcast_to(level2, (8, 128))
+
+        def reforce(k, _):
+            for half in range(2):
+                force[k, half] = level2 * src[k, half]
+            return 0
+
+        lax.fori_loop(0, EXT, reforce, 0, unroll=4)
+
         @pl.when(has_low)
         def _():
             halo2(1).wait_recv()
-            ghost_mean(1).wait_recv()
+            for part in range(2):
+                ghost_copy(part, 1).wait_recv()
 
         @pl.when(has_high)
         def _():
             halo2(0).wait_recv()
-            ghost_mean(0).wait_recv()
-
-        low_wide = {r: unpack(cghost[0, r:r + 1, :]) for r in (1, 2, 3)}
-        high_wide = {r: unpack(cghost[1, r:r + 1, :]) for r in (0, 1, 2)}
+            for part in range(2):
+                ghost_copy(part, 0).wait_recv()
+
+        low_wide = {r: unpack(ghost[0, 0, r:r + 1, :] + ghost[1, 0, r:r + 1, :]) for r in (1, 2, 3)}
+        high_wide = {r: unpack(ghost[0, 1, r:r + 1, :] + ghost[1, 1, r:r + 1, :]) for r in (0, 1, 2)}
         for i in range(HALO):
             for half in range(2):
                 u[i, half] = dhalo[0, i, half] + low_wide[(LAYERS - HALO + i) // 4]
@@ -407,9 +448,9 @@
         jump = end_mean - decay * coarse
         final_copy = pltpu.make_async_remote_copy(
             src_ref=u.at[own], dst_ref=fin, send_sem=f_send, recv_sem=f_recv,
-            device_id=t_peer(2), device_id_type=MESH,
+            device_id=(last, slab), device_id_type=MESH,
         )
-        coarse, sends = coarse_solve(1, jump, 2, final_copy.start)
+        coarse, sends = coarse_solve(1, jump, final_copy.start)
         pending += sends
         wides = [unpack(coarse[zc:zc + 1]) for zc in range(4)]
         final_copy.wait_recv()
@@ -422,19 +463,20 @@
         for copy in pending:
             copy.wait_send()
         final_copy.wait_send()
-        level_copy.wait_send()
 
         @pl.when(has_high)
         def _():
             for copy in halo_copies(1):
                 copy.wait_send()
-            ghost_mean(1).wait_send()
+            for part in range(2):
+                ghost_copy(part, 1).wait_send()
 
         @pl.when(has_low)
         def _():
             for copy in halo_copies(0):
                 copy.wait_send()
-            ghost_mean(0).wait_send()
+            for part in range(2):
+                ghost_copy(part, 0).wait_send()
 
     return kernel
 
@@ -445,6 +487,7 @@
     hbm = pl.BlockSpec(memory_space=pl.ANY)
     vmem = pl.BlockSpec(memory_space=pltpu.VMEM)
     dma = pltpu.SemaphoreType.DMA
+    regular = pltpu.SemaphoreType.REGULAR
     field = pltpu.VMEM((EXT, 2, 8, 128), f32)
     return pl.pallas_call(
         make_kernel(),
@@ -456,19 +499,18 @@
             pltpu.VMEM((EXT, 16, 128), jnp.int32),
             pltpu.VMEM((EXT, 16, 128), f32),
             field, field, field, field,
+            pltpu.VMEM((2, 32, 8, 128), f32),
             pltpu.VMEM((2, 8, 128), f32),
-            pltpu.VMEM((2, 8, 4, 128), f32),
-            pltpu.VMEM((2, 8, 4, 128), f32),
-            pltpu.VMEM((2, 8, 4, 128), f32),
-            pltpu.VMEM((WINDOWS, 4, 128), f32),
+            pltpu.VMEM((2, 8, 128), f32),
             pltpu.VMEM((4, 128), f32),
-            pltpu.VMEM((2, 4, 128), f32),
+            pltpu.VMEM((2, 2, 4, 128), f32),
+            pltpu.VMEM((2, 2, 32, 4, 128), f32),
             pltpu.VMEM((2, HALO, 2, 8, 128), f32),
             pltpu.VMEM((LAYERS, 2, 8, 128), f32),
             dma((3,)), dma((2, 3)), dma((2, 3)),
-            dma((2, 8)), dma((2, 8)), dma((2, 8)), dma((2, 8)),
-            dma((2,)), dma((2,)), dma((2,)), dma((2,)),
-            dma(()), dma(()), dma(()), dma(()),
+            dma((2, 32)), dma((2, 32)), dma((2,)), dma((2,)),
+            dma((2,)), dma((2,)), dma((2, 2)), dma((2, 2)),
+            dma(()), dma(()), regular, regular, regular, regular,
         ],
         compiler_params=pltpu.CompilerParams(collective_id=0, has_side_effects=True),
     )(start_states, material, source, conductivity, tide_amp, phase, coarse_rate)

time: 53.1 us -> 49.9 us (0.940)
  Pallas kernels: 50.7 us -> 47.5 us
    pallas_call x1, Pallas kernels: 50.7 us -> 47.5 us  [body(): pl.pallas_call(make_kernel(), out_shape=jax.ShapeDtypeStruct((1, LAYERS,...]
where the time goes in v2:
time: 49.9 us; the launch traced here: 49.7 us
  Pallas kernels  47.5 us (95%)
  local copies, waits for them, and re-layouts  1.57 us (3%)
  between operations  0.66 us (1%)
    pallas_call x1, Pallas kernels, body(): pl.pallas_call(make_kernel(), out_shape=jax.ShapeDtypeStruct((1, LAYERS,...  47.5 us
    unnamed x1, local copies, waits for them, and re-layouts  1.57 us

profile of v2, /device:TPU:1, one launch (start us, length us, event | category | flops | bytes accessed | tf_op | source)
XLA Modules:
  0.0 49.7 jit_solution(9916140359976156909)
XLA Ops:
  0.7 47.5 %shard_map.73 = f32[1,16,16,128]{3,2,1,0:T(8,128)} custom-call(f32[1,16,16,128]{3,2,1,0:T(8,128)} %start.1, s32[16,16,128]{2,1,0:T(8,128)} %material.1, f32[16,16,128]{2,1,0:T(8,128)} %source.1, f32[16]{0:T(128)} %cond.1, f32[12]{0:T(128)} %amp.1, s32[1]{0:T(128)S(6)} %copy.9.phase, f32[4,4,32]{2,1,0:T(4,128)} %rate.1), custom_call_target="tpu_custom_call" | custom-call | tf_op jit(solution)/shard_map/pallas_call | solution.py:492
  48.2 1.6 %copy.10 = f32[1,16,16,128]{3,2,1,0:T(8,128)} copy(f32[1,16,16,128]{3,2,1,0:T(8,128)} %shard_map.73) | data formatting | bytes 262144

commit v3 on v2

--- a/solution.py
+++ b/solution.py
@@ -12,7 +12,6 @@
 HALO = FINE
 EXT = LAYERS + 2 * HALO
 MESH = pl.DeviceIdType.MESH
-GROUPS = ((1, 3), (4, 3), (7, 4))
 
 
 def roll(x, shift, axis):
@@ -21,7 +20,8 @@
 
 def make_kernel():
     def kernel(
-        start, material, source, cond, amp, phase, rate, out,
+        start, material, source, cond_in, amp_in, phase_in, rate_in, out,
+        cond, amp, phase, rate, low_edge, high_edge,
         nat_u, nat_m, nat_s, u, coef, force, src, jbuf, ksend, kbuf, tsend,
         ghost, weight, dhalo, fin,
         loc_sem, h_send, h_recv, j_send, j_recv, k_send, k_recv,
@@ -44,41 +44,40 @@
         twin = (twin_tm, slab)
         last = lax.rem(tm + 2, WINDOWS)
 
+        barrier = pltpu.get_barrier_semaphore()
+
+        def greet(peer):
+            pl.semaphore_signal(barrier, inc=1, device_id=peer, device_id_type=MESH)
+
+        @pl.when(has_low)
+        def _():
+            greet((tm, slab - 1))
+
+        @pl.when(has_high)
+        def _():
+            greet((tm, slab + 1))
+
+        for dx, dy in ((0, 1), (0, 7), (1, 0), (3, 0)):
+            greet(plane_peer(dx, dy))
+
+        @pl.when(zz == 0)
+        def _():
+            greet(twin)
+
         own = pl.ds(HALO, LAYERS)
+        small = [(phase_in, phase), (amp_in, amp), (cond_in, cond), (rate_in, rate)]
+        small = [pltpu.make_async_copy(a, b, loc_sem.at[3 + i]) for i, (a, b) in enumerate(small)]
         locals_ = [
             pltpu.make_async_copy(start.at[0], nat_u.at[own], loc_sem.at[0]),
             pltpu.make_async_copy(material, nat_m.at[own], loc_sem.at[1]),
             pltpu.make_async_copy(source, nat_s.at[own], loc_sem.at[2]),
         ]
-        for copy in locals_:
+        for copy in small + locals_:
             copy.start()
-
-        barrier = pltpu.get_barrier_semaphore()
-
-        def greet(peer):
-            pl.semaphore_signal(barrier, inc=1, device_id=peer, device_id_type=MESH)
-
-        @pl.when(has_low)
-        def _():
-            greet((tm, slab - 1))
-
-        @pl.when(has_high)
-        def _():
-            greet((tm, slab + 1))
-
-        for dx, dy in ((0, 1), (0, 7), (1, 0), (3, 0)):
-            greet(plane_peer(dx, dy))
-
-        @pl.when(zz == 0)
-        def _():
-            greet(twin)
 
         def tell(sem, peers):
             for peer in peers:
                 pl.semaphore_signal(sem, inc=1, device_id=peer, device_id_type=MESH)
-
-        level_own = amp[phase[0]]
-        jbuf[0, 0, 4:8, :] = jnp.full((4, 128), level_own, jnp.float32)
 
         sides = jnp.where(has_low, 1, 0) + jnp.where(has_high, 1, 0)
         pl.semaphore_wait(barrier, 4 + sides + zz)
@@ -165,6 +164,11 @@
         @pl.when(jnp.logical_not(has_high))
         def _():
             clear(1)
+
+        for copy in small:
+            copy.wait()
+        level_own = amp[phase[0]]
+        jbuf[0, 0, 4:8, :] = jnp.full((4, 128), level_own, jnp.float32)
 
         spread_row = lax.broadcasted_iota(jnp.int32, (32, 128), 0)
         spread_col = lax.broadcasted_iota(jnp.int32, (32, 128), 1)
@@ -193,9 +197,7 @@
                     weight[it, half, i] = jnp.exp(step_rate * power.astype(jnp.float32)) * unclose
                 return 0
 
-            lax.fori_loop(0, 32, go, 0, unroll=2)
-
-        powers(0)
+            lax.fori_loop(0, 32, go, 0, unroll=4)
 
         def lookup(m):
             picks = [cond[i] for i in range(16)]
@@ -224,10 +226,10 @@
 
             lax.fori_loop(0, count, go, 0, unroll=2)
 
+        for copy in locals_:
+            copy.wait()
         pl.semaphore_wait(near, 4)
         tell(ring, tuple(plane_peer(dx, dy) for dx, dy in ((0, 2), (0, 6), (1, 0), (3, 0))))
-        for copy in locals_:
-            copy.wait()
         arrange(HALO, LAYERS, None)
 
         def slab_means():
@@ -241,6 +243,53 @@
 
         start_mean = pack(slab_means())
 
+        def advance(k, before, here, after):
+            even, odd = here
+            across = (
+                odd + jnp.where(first_sub, zero, roll(odd, 1, 0)),
+                even + jnp.where(last_sub, zero, roll(even, -1, 0)),
+            )
+            for half in range(2):
+                now = here[half]
+                total = before[half] + after[half] + across[half]
+                total = total + jnp.where(first_lane, zero, roll(now, 1, 1))
+                total = total + jnp.where(last_lane, zero, roll(now, -1, 1))
+                u[k, half] = now + coef[k, half] * (total - 6.0 * now) + force[k, half]
+
+        def layer(ref, k):
+            return ref[k, 0], ref[k, 1]
+
+        def sweep(base, lo, hi, below=None, above=None):
+            before = below if below is not None else layer(u, base + lo - 1)
+            here = layer(u, base + lo)
+            for k in range(lo, hi):
+                after = above if above is not None and k == hi - 1 else layer(u, base + k + 1)
+                advance(base + k, before, here, after)
+                before, here = here, after
+
+        def inner():
+            for t in range(1, 8):
+                lo, hi = HALO + t, HALO + LAYERS - t
+                for half in range(2):
+                    low_edge[t, half] = u[lo, half]
+                    high_edge[t, half] = u[hi - 1, half]
+                sweep(0, lo, hi)
+
+        def outer():
+            for t in range(1, 8):
+                sweep(0, t, HALO + t, above=layer(low_edge, t))
+                sweep(0, EXT - HALO - t, EXT - t, below=layer(high_edge, t))
+
+            def rest(i, _):
+                sweep(0, 8, EXT - 8)
+                return 0
+
+            lax.fori_loop(0, 3, rest, 0)
+
+        inner()
+        pl.semaphore_wait(ring, 4)
+        tell(cross, (plane_peer(0, 2), plane_peer(0, 6)))
+
         @pl.when(has_low)
         def _():
             for copy in halo_copies(1):
@@ -254,48 +303,21 @@
         arrange(0, HALO, jnp.where(has_low, 1.0, 0.0))
         arrange(HALO + LAYERS, HALO, jnp.where(has_high, 1.0, 0.0))
 
-        def sweep(lo, hi):
-            before = (u[lo - 1, 0], u[lo - 1, 1])
-            here = (u[lo, 0], u[lo, 1])
-            for k in range(lo, hi):
-                after = (u[k + 1, 0], u[k + 1, 1])
-                even, odd = here
-                across = (
-                    odd + jnp.where(first_sub, zero, roll(odd, 1, 0)),
-                    even + jnp.where(last_sub, zero, roll(even, -1, 0)),
-                )
-                for half in range(2):
-                    now = here[half]
-                    total = before[half] + after[half] + across[half]
-                    total = total + jnp.where(first_lane, zero, roll(now, 1, 1))
-                    total = total + jnp.where(last_lane, zero, roll(now, -1, 1))
-                    u[k, half] = now + coef[k, half] * (total - 6.0 * now) + force[k, half]
-                before, here = here, after
-
-        def fine():
-            for first, count in GROUPS:
-                def go(i, _):
-                    sweep(first, EXT - first)
-                    return 0
-
-                lax.fori_loop(0, count, go, 0)
+        def pl_all(it, rows, sem):
+            every = jbuf.at[it, pl.ds(1, 31), rows]
+            return pltpu.make_async_copy(every, every, sem.at[it])
 
         def coarse_solve(it, jump, between):
             rows = pl.ds(0, 8 if it == 0 else 4)
             jbuf[it, 0, 0:4, :] = jump
-            sends = []
             for dx, dy in peers:
-                slot = 8 * dx + dy
-                copy = pltpu.make_async_remote_copy(
-                    src_ref=jbuf.at[it, 0, rows], dst_ref=jbuf.at[it, slot, rows],
-                    send_sem=j_send.at[it, slot], recv_sem=j_recv.at[it, slot],
+                pltpu.make_async_remote_copy(
+                    src_ref=jbuf.at[it, 0, rows], dst_ref=jbuf.at[it, 8 * dx + dy, rows],
+                    send_sem=j_send.at[it], recv_sem=j_recv.at[it],
                     device_id=plane_peer(dx, dy), device_id_type=MESH,
-                )
-                copy.start()
-                sends.append(copy)
+                ).start()
             between()
-            for copy in sends:
-                copy.wait_recv()
+            pl_all(it, rows, j_recv).wait()
 
             def weigh(half):
                 terms = [weight[it, half, i] * jbuf[it, i, 0:4, :] for i in range(32)]
@@ -312,7 +334,6 @@
                 device_id=twin, device_id_type=MESH,
             )
             copy.start()
-            sends.append(copy)
             if it == 0:
                 ghost_step(0)
             total = weigh(0)
@@ -320,7 +341,7 @@
                 tsend[...] = total
                 ghost_step(1)
             copy.wait_recv()
-            return total + kbuf[it, 0:4, :], sends
+            return total + kbuf[it, 0:4, :], [copy]
 
         def ghost_copy(part, side):
             target = (twin_tm if part == 0 else tm, slab - 1 if side == 0 else slab + 1)
@@ -345,7 +366,7 @@
             key=lambda p: -min(p[0], 4 - p[0]) - min(p[1], 8 - p[1]),
         )
         pending = []
-        fine()
+        outer()
 
         def detach():
             means = slab_means()
@@ -377,19 +398,17 @@
             def _():
                 halo2(0).start()
 
+            powers(0)
             powers(1)
+
+            @pl.when(zz == 0)
+            def _():
+                pl.semaphore_wait(up, 1)
+                tell(up, (twin,))
 
             @pl.when(zz == 1)
             def _():
                 pl.semaphore_wait(up, 1)
-
-        pl.semaphore_wait(ring, 4)
-        tell(cross, (plane_peer(0, 2), plane_peer(0, 6)))
-
-        @pl.when(zz == 0)
-        def _():
-            pl.semaphore_wait(up, 1)
-            tell(up, (twin,))
 
         pl.semaphore_wait(cross, 2)
         coarse, sends = coarse_solve(0, jump, between1)
@@ -422,6 +441,7 @@
             return 0
 
         lax.fori_loop(0, EXT, reforce, 0, unroll=4)
+        inner()
 
         @pl.when(has_low)
         def _():
@@ -442,7 +462,7 @@
                 u[i, half] = dhalo[0, i, half] + low_wide[(LAYERS - HALO + i) // 4]
                 u[HALO + LAYERS + i, half] = dhalo[1, i, half] + high_wide[i // 4]
 
-        fine()
+        outer()
 
         end_mean = detach()
         jump = end_mean - decay * coarse
@@ -462,6 +482,8 @@
 
         for copy in pending:
             copy.wait_send()
+        pl_all(0, pl.ds(0, 8), j_send).wait()
+        pl_all(1, pl.ds(0, 4), j_send).wait()
         final_copy.wait_send()
 
         @pl.when(has_high)
@@ -483,7 +505,6 @@
 
 def body(start_states, material, source, conductivity, tide_amp, phase, coarse_rate):
     f32 = jnp.float32
-    smem = pl.BlockSpec(memory_space=pltpu.SMEM)
     hbm = pl.BlockSpec(memory_space=pl.ANY)
     vmem = pl.BlockSpec(memory_space=pltpu.VMEM)
     dma = pltpu.SemaphoreType.DMA
@@ -492,9 +513,15 @@
     return pl.pallas_call(
         make_kernel(),
         out_shape=jax.ShapeDtypeStruct((1, LAYERS, 16, 128), f32),
-        in_specs=[hbm, hbm, hbm, smem, smem, smem, vmem],
+        in_specs=[hbm] * 7,
         out_specs=vmem,
         scratch_shapes=[
+            pltpu.SMEM((16,), f32),
+            pltpu.SMEM((12,), f32),
+            pltpu.SMEM((1,), jnp.int32),
+            pltpu.VMEM((4, 4, 32), f32),
+            pltpu.VMEM((8, 2, 8, 128), f32),
+            pltpu.VMEM((8, 2, 8, 128), f32),
             pltpu.VMEM((EXT, 16, 128), f32),
             pltpu.VMEM((EXT, 16, 128), jnp.int32),
             pltpu.VMEM((EXT, 16, 128), f32),
@@ -507,8 +534,8 @@
             pltpu.VMEM((2, 2, 32, 4, 128), f32),
             pltpu.VMEM((2, HALO, 2, 8, 128), f32),
             pltpu.VMEM((LAYERS, 2, 8, 128), f32),
-            dma((3,)), dma((2, 3)), dma((2, 3)),
-            dma((2, 32)), dma((2, 32)), dma((2,)), dma((2,)),
+            dma((7,)), dma((2, 3)), dma((2, 3)),
+            dma((2,)), dma((2,)), dma((2,)), dma((2,)),
             dma((2,)), dma((2,)), dma((2, 2)), dma((2, 2)),
             dma(()), dma(()), regular, regular, regular, regular,
         ],

time: 49.9 us -> 44.2 us (0.89)
  Pallas kernels: 47.5 us -> 41.9 us
    pallas_call x1, Pallas kernels: 47.5 us -> 41.9 us  [body(): pl.pallas_call(make_kernel(), out_shape=jax.ShapeDtypeStruct((1, LAYERS,...]
where the time goes in v3:
time: 44.2 us; the launch traced here: 44.1 us
  Pallas kernels  41.9 us (95%)
  local copies, waits for them, and re-layouts  1.57 us (4%)
  between operations  0.66 us (1%)
    pallas_call x1, Pallas kernels, body(): pl.pallas_call(make_kernel(), out_shape=jax.ShapeDtypeStruct((1, LAYERS,...  41.9 us
    unnamed x1, local copies, waits for them, and re-layouts  1.57 us

profile of v3, /device:TPU:1, one launch (start us, length us, event | category | flops | bytes accessed | tf_op | source)
XLA Modules:
  0.0 44.1 jit_solution(995471937475389277)
XLA Ops:
  0.7 41.9 %shard_map.73 = f32[1,16,16,128]{3,2,1,0:T(8,128)} custom-call(f32[1,16,16,128]{3,2,1,0:T(8,128)} %start.1, s32[16,16,128]{2,1,0:T(8,128)} %material.1, f32[16,16,128]{2,1,0:T(8,128)} %source.1, f32[16]{0:T(128)} %cond_in.1, f32[12]{0:T(128)} %amp_in.1, s32[1]{0:T(128)S(6)} %copy.9.phase_in, f32[4,4,32]{2,1,0:T(4,128)} %rate_in.1), custom_call_target="tpu_custom_call" | custom-call | tf_op jit(solution)/shard_map/pallas_call | solution.py:513
  42.5 1.6 %copy.10 = f32[1,16,16,128]{3,2,1,0:T(8,128)} copy(f32[1,16,16,128]{3,2,1,0:T(8,128)} %shard_map.73) | data formatting | bytes 262144

commit v4 on v3

--- a/solution.py
+++ b/solution.py
@@ -10,6 +10,7 @@
 SLABS = 8
 LAYERS = 16
 HALO = FINE
+VMEM_BYTES = 16 * 2**20
 EXT = LAYERS + 2 * HALO
 MESH = pl.DeviceIdType.MESH
 
@@ -21,11 +22,11 @@
 def make_kernel():
     def kernel(
         start, material, source, cond_in, amp_in, phase_in, rate_in, out,
-        cond, amp, phase, rate, low_edge, high_edge,
+        cond, amp, phase, rate, result, low_edge, high_edge,
         nat_u, nat_m, nat_s, u, coef, force, src, jbuf, ksend, kbuf, tsend,
         ghost, weight, dhalo, fin,
         loc_sem, h_send, h_recv, j_send, j_recv, k_send, k_recv,
-        d_send, d_recv, g_send, g_recv, f_send, f_recv, near, ring, cross, up,
+        d_send, d_recv, g_send, g_recv, f_send, f_recv, f_out, near, ring, cross, up,
     ):
         tm = lax.axis_index("tm")
         slab = lax.axis_index("space")
@@ -478,13 +479,17 @@
             for i in range(4):
                 k = 4 * zc + i
                 for half in range(2):
-                    out[0, k, pl.ds(half, 8, stride=2), :] = fin[k, half] + wides[zc]
+                    result[k, pl.ds(half, 8, stride=2), :] = fin[k, half] + wides[zc]
+
+        result_copy = pltpu.make_async_copy(result, out.at[0], f_out)
+        result_copy.start()
 
         for copy in pending:
             copy.wait_send()
         pl_all(0, pl.ds(0, 8), j_send).wait()
         pl_all(1, pl.ds(0, 4), j_send).wait()
         final_copy.wait_send()
+        result_copy.wait()
 
         @pl.when(has_high)
         def _():
@@ -505,8 +510,8 @@
 
 def body(start_states, material, source, conductivity, tide_amp, phase, coarse_rate):
     f32 = jnp.float32
-    hbm = pl.BlockSpec(memory_space=pl.ANY)
-    vmem = pl.BlockSpec(memory_space=pltpu.VMEM)
+    hbm = pl.BlockSpec(memory_space=pltpu.HBM)
+    somewhere = pl.BlockSpec(memory_space=pl.ANY)
     dma = pltpu.SemaphoreType.DMA
     regular = pltpu.SemaphoreType.REGULAR
     field = pltpu.VMEM((EXT, 2, 8, 128), f32)
@@ -514,12 +519,13 @@
         make_kernel(),
         out_shape=jax.ShapeDtypeStruct((1, LAYERS, 16, 128), f32),
         in_specs=[hbm] * 7,
-        out_specs=vmem,
+        out_specs=somewhere,
         scratch_shapes=[
             pltpu.SMEM((16,), f32),
             pltpu.SMEM((12,), f32),
             pltpu.SMEM((1,), jnp.int32),
             pltpu.VMEM((4, 4, 32), f32),
+            pltpu.VMEM((LAYERS, 16, 128), f32),
             pltpu.VMEM((8, 2, 8, 128), f32),
             pltpu.VMEM((8, 2, 8, 128), f32),
             pltpu.VMEM((EXT, 16, 128), f32),
@@ -537,10 +543,19 @@
             dma((7,)), dma((2, 3)), dma((2, 3)),
             dma((2,)), dma((2,)), dma((2,)), dma((2,)),
             dma((2,)), dma((2,)), dma((2, 2)), dma((2, 2)),
-            dma(()), dma(()), regular, regular, regular, regular,
+            dma(()), dma(()), dma(()), regular, regular, regular, regular,
         ],
-        compiler_params=pltpu.CompilerParams(collective_id=0, has_side_effects=True),
-    )(start_states, material, source, conductivity, tide_amp, phase, coarse_rate)
+        compiler_params=pltpu.CompilerParams(
+            collective_id=0, has_side_effects=True, vmem_limit_bytes=VMEM_BYTES
+        ),
+    )(
+        *(
+            pltpu.with_memory_space_constraint(x, pltpu.HBM)
+            for x in (start_states, material, source, conductivity, tide_amp)
+        ),
+        phase,
+        pltpu.with_memory_space_constraint(coarse_rate, pltpu.HBM),
+    )
 
 
 def solution(mesh):

time: 44.2 us -> 42.9 us (0.971)
  local copies, waits for them, and re-layouts: 1.57 us -> 0.66 us
  Pallas kernels: 41.9 us -> 41.4 us
    unnamed x1, local copies, waits for them, and re-layouts: 1.57 us -> 0.66 us
where the time goes in v4:
time: 42.9 us; the launch traced here: 42.7 us
  Pallas kernels  41.4 us (97%)
  local copies, waits for them, and re-layouts  0.66 us (2%)
  between operations  0.66 us (2%)
    pallas_call x1, Pallas kernels, body(): pl.pallas_call(make_kernel(), out_shape=jax.ShapeDtypeStruct((1, LAYERS,...  41.4 us

profile of v4, /device:TPU:1, one launch (start us, length us, event | category | flops | bytes accessed | tf_op | source)
XLA Modules:
  0.0 42.7 jit_solution(16032222941136402052)
XLA Ops:
  0.7 41.4 %shard_map.73 = f32[1,16,16,128]{3,2,1,0:T(8,128)S(1)} custom-call(f32[1,16,16,128]{3,2,1,0:T(8,128)} %start.1, s32[16,16,128]{2,1,0:T(8,128)} %material.1, f32[16,16,128]{2,1,0:T(8,128)} %source.1, f32[16]{0:T(128)} %cond_in.1, f32[12]{0:T(128)} %amp_in.1, s32[1]{0:T(128)S(6)} %copy.9.phase_in, f32[4,4,32]{2,1,0:T(4,128)} %rate_in.1), custom_call_target="tpu_custom_call" | custom-call | tf_op jit(solution)/shard_map/pallas_call | solution.py:518
  42.1 0.7 %copy.10 = f32[1,16,16,128]{3,2,1,0:T(8,128)} copy(f32[1,16,16,128]{3,2,1,0:T(8,128)S(1)} %shard_map.73) | data formatting | bytes 262144

commit v5 on v4

--- a/solution.py
+++ b/solution.py
@@ -474,22 +474,25 @@
         coarse, sends = coarse_solve(1, jump, final_copy.start)
         pending += sends
         wides = [unpack(coarse[zc:zc + 1]) for zc in range(4)]
+        def result_copy(zc):
+            part = pl.ds(4 * zc, 4)
+            return pltpu.make_async_copy(result.at[part], out.at[0, part], f_out.at[zc])
+
         final_copy.wait_recv()
         for zc in range(4):
             for i in range(4):
                 k = 4 * zc + i
                 for half in range(2):
                     result[k, pl.ds(half, 8, stride=2), :] = fin[k, half] + wides[zc]
-
-        result_copy = pltpu.make_async_copy(result, out.at[0], f_out)
-        result_copy.start()
+            result_copy(zc).start()
 
         for copy in pending:
             copy.wait_send()
         pl_all(0, pl.ds(0, 8), j_send).wait()
         pl_all(1, pl.ds(0, 4), j_send).wait()
         final_copy.wait_send()
-        result_copy.wait()
+        for zc in range(4):
+            result_copy(zc).wait()
 
         @pl.when(has_high)
         def _():
@@ -543,7 +546,7 @@
             dma((7,)), dma((2, 3)), dma((2, 3)),
             dma((2,)), dma((2,)), dma((2,)), dma((2,)),
             dma((2,)), dma((2,)), dma((2, 2)), dma((2, 2)),
-            dma(()), dma(()), dma(()), regular, regular, regular, regular,
+            dma(()), dma(()), dma((4,)), regular, regular, regular, regular,
         ],
         compiler_params=pltpu.CompilerParams(
             collective_id=0, has_side_effects=True, vmem_limit_bytes=VMEM_BYTES

time: 42.9 us -> 42.9 us (level)
  no operation moved by 1% of the time
where the time goes in v5:
time: 42.9 us; the launch traced here: 42.7 us
  Pallas kernels  41.4 us (97%)
  local copies, waits for them, and re-layouts  0.66 us (2%)
  between operations  0.66 us (2%)
    pallas_call x1, Pallas kernels, body(): pl.pallas_call(make_kernel(), out_shape=jax.ShapeDtypeStruct((1, LAYERS,...  41.4 us

profile of v5, /device:TPU:1, one launch (start us, length us, event | category | flops | bytes accessed | tf_op | source)
XLA Modules:
  0.0 42.7 jit_solution(17496817902173078696)
XLA Ops:
  0.7 41.4 %shard_map.73 = f32[1,16,16,128]{3,2,1,0:T(8,128)S(1)} custom-call(f32[1,16,16,128]{3,2,1,0:T(8,128)} %start.1, s32[16,16,128]{2,1,0:T(8,128)} %material.1, f32[16,16,128]{2,1,0:T(8,128)} %source.1, f32[16]{0:T(128)} %cond_in.1, f32[12]{0:T(128)} %amp_in.1, s32[1]{0:T(128)S(6)} %copy.9.phase_in, f32[4,4,32]{2,1,0:T(4,128)} %rate_in.1), custom_call_target="tpu_custom_call" | custom-call | tf_op jit(solution)/shard_map/pallas_call | solution.py:521
  42.1 0.7 %copy.10 = f32[1,16,16,128]{3,2,1,0:T(8,128)} copy(f32[1,16,16,128]{3,2,1,0:T(8,128)S(1)} %shard_map.73) | data formatting | bytes 262144
